TPU v7x, 32 devices: a whole 2x2x4 slice. The times are simulated.
32 devices in a mesh: seq: 16 (over z, y, x), head: 2 (over core).
Axes of the slice: x: 2, y: 2, z: 4, core: 2. Of those that a mesh axis runs over, the one named last changes fastest.
Arguments:
- block_in: bfloat16 [8192, 768], P(('seq', 'head')), may hold values from -6 to 6
- grad_out: bfloat16 [8192, 768], P(('seq', 'head')), may hold values from -6 to 6
- lengths: int32 [2], replicated, may hold values from 1024 to 4096, as said below
- norm_gain: float32 [768], replicated, may hold values from 0.25 to 1.75
- w_in: bfloat16 [768, 3352], replicated, may hold values from -0.21875 to 0.21875
- conv_w: float32 [4, 1792], replicated, may hold values from -3 to 3
- conv_b: float32 [1792], replicated, may hold values from -0.5 to 0.5
- dt_bias: float32 [24], replicated, may hold values from -6 to -3.5
- a_log: float32 [24], replicated, may hold values from -10.5 to 1.4
- d_skip: float32 [24], replicated, may hold values from 0.5 to 2
- gate_gain: float32 [1536], replicated, may hold values from 0.25 to 1.75
- w_out: bfloat16 [1536, 768], replicated, may hold values from -0.15625 to 0.15625
Outputs:
- block_out: bfloat16 [8192, 768], P(('seq', 'head'))
- grad_in: float32 [8192, 768], P(('seq', 'head'))
- grad_norm_gain: float32 [768], replicated
- grad_w_in: float32 [768, 3352], replicated
- grad_conv_w: float32 [4, 1792], replicated
- grad_conv_b: float32 [1792], replicated
- grad_dt_bias: float32 [24], replicated
- grad_a_log: float32 [24], replicated
- grad_d_skip: float32 [24], replicated
- grad_gate_gain: float32 [1536], replicated
- grad_w_out: float32 [1536, 768], replicated
Inputs may be any that keep to these rules, and one draw needn't show every extreme that they name: lengths[s] counts the valid slots at the start of sequence s, the rest being padding; at least one sequence is valid in all 4096 slots.
All inputs are finite; a program needn't handle non-finite values.
Results may differ from a plain program's by a relative error of at most 0.012.
The roundings to bfloat16 on the way count: a program that leaves them out, or rounds other values in their place, can miss the bound.
Values may be sent and summed in bfloat16 or wider, within the bound.
A program may use at most 320 MiB of HBM per device.

v0:
```python
from functools import partial
import jax
import jax.numpy as jnp
from jax import lax
from jax.sharding import PartitionSpec as P

INNER = 1536
HEADS = 24
HEAD_DIM = 64
STATE = 128
CONV = 4
BLOCK = 256
SEQS = 2
eps_norm = 1e-05
best = lax.Precision.HIGHEST


def passed_along(value, axis, steps):
    count = lax.axis_size(axis)
    initial, last = (max(0, -steps), min(count, count - steps))
    return lax.ppermute(value, axis, [(source, source + steps) for source in range(initial, last)])


def entering(part, axis, combine, identity, reverse):
    count = lax.axis_size(axis)
    place = lax.axis_index(axis)
    ahead = count - 1 - place if reverse else place
    gathered = jax.tree.map(lambda a: lax.all_gather(a, axis), part)
    state = jax.tree.map(lambda a, e: jnp.zeros_like(a) + jnp.asarray(e, a.dtype), part, identity)

    def one(turn, state):
        source = count - 1 - turn if reverse else turn
        return combine(
            state, jax.tree.map(lambda a: lax.dynamic_index_in_dim(a, source, 0, False), gathered)
        )

    return lax.fori_loop(0, ahead, one, state)


def inverse_rms(values):
    return lax.rsqrt(jnp.mean(values * values, axis=-1, keepdims=True) + eps_norm)


def norm_backward(values, scaling, gain_vec, gradient):
    weighted = gradient * gain_vec
    average = jnp.mean(weighted * values, axis=-1, keepdims=True)
    grad_values = scaling * weighted - values * (scaling * scaling * scaling) * average
    grad_gain = jnp.sum(gradient * values * scaling, axis=0)
    return (grad_values, grad_gain)


def causal_conv(edge_rows, fresh_rows, weights, offset):
    length = fresh_rows.shape[0]
    joined = jnp.concatenate([edge_rows, fresh_rows], axis=0)
    running = offset + joined[0:length] * weights[0]
    for position in range(1, CONV):
        running = running + joined[position : position + length] * weights[position]
    return running


def prepare(
    x_raw,
    bc_raw,
    dt_raw,
    edge_x,
    edge_bc,
    conv_x,
    conv_bc,
    bias_x,
    bias_bc,
    dt_shift,
    a_log_part,
    valid_mask,
):
    keep_mask = valid_mask[:, None]
    x_flat = jax.nn.silu(causal_conv(edge_x, x_raw, conv_x, bias_x)) * keep_mask
    act_bc = jax.nn.silu(causal_conv(edge_bc, bc_raw, conv_bc, bias_bc))
    dt_rows = jax.nn.softplus(dt_raw + dt_shift) * keep_mask
    rates = -jnp.exp(a_log_part)
    x_heads = x_flat.reshape(x_flat.shape[0], -1, HEAD_DIM)
    return (x_heads, act_bc[:, :STATE], act_bc[:, STATE:], dt_rows, rates)


def block_step(rates, carry_state, inputs):
    x_heads, b_rows, c_rows, dt_rows = inputs
    block_len = dt_rows.shape[0]
    cumulative = jnp.cumsum(dt_rows, axis=0) * rates
    indices = jnp.arange(block_len)
    causal = (indices[:, None] >= indices[None, :])[:, :, None]
    spread = cumulative[:, None, :] - cumulative[None, :, :]
    decays = jnp.where(causal, jnp.exp(jnp.where(causal, spread, 0.0)), 0.0)
    scores = jnp.dot(c_rows, b_rows.T, precision=best)
    weight = decays * scores[:, :, None] * dt_rows[None, :, :]
    inner_part = jnp.einsum("tuh,uhp->thp", weight, x_heads, precision=best)
    carried = jnp.exp(cumulative)[:, :, None] * jnp.einsum(
        "tn,hpn->thp", c_rows, carry_state, precision=best
    )
    to_end = jnp.exp(cumulative[-1:] - cumulative) * dt_rows
    fresh_state = jnp.einsum("uh,uhp,un->hpn", to_end, x_heads, b_rows, precision=best)
    carry_state = jnp.exp(cumulative[-1])[:, None, None] * carry_state + fresh_state
    return (carry_state, inner_part + carried)


def mixer(
    valid_mask,
    x_raw,
    bc_raw,
    dt_raw,
    edge_x,
    edge_bc,
    conv_x,
    conv_bc,
    bias_x,
    bias_bc,
    dt_shift,
    a_log_part,
    skip_part,
    incoming,
):
    x_heads, b_rows, c_rows, dt_rows, rates = prepare(
        x_raw,
        bc_raw,
        dt_raw,
        edge_x,
        edge_bc,
        conv_x,
        conv_bc,
        bias_x,
        bias_bc,
        dt_shift,
        a_log_part,
        valid_mask,
    )
    blocks_count = x_heads.shape[0] // BLOCK

    def blocks(values):
        return values.reshape((blocks_count, BLOCK) + values.shape[1:])

    final_state, outputs = lax.scan(
        partial(block_step, rates),
        incoming,
        (blocks(x_heads), blocks(b_rows), blocks(c_rows), blocks(dt_rows)),
    )
    mixed_rows = outputs.reshape(x_heads.shape) + x_heads * skip_part[:, None]
    return (mixed_rows.reshape(x_heads.shape[0], -1), final_state)


def chain(earlier, later):
    return (earlier[0] * later[0], later[0][..., None, None] * earlier[1] + later[1])


def place_into(piece, full_len, start):
    full_shape = piece.shape[:-1] + (full_len,)
    return lax.dynamic_update_slice_in_dim(
        jnp.zeros(full_shape, jnp.float32), piece, start, piece.ndim - 1
    )


def local(
    block_in,
    grad_out,
    lengths,
    norm_gain,
    w_in,
    conv_w,
    conv_b,
    dt_bias,
    a_log,
    d_skip,
    gate_gain,
    w_out,
):
    tokens = block_in.shape[0]
    groups = lax.axis_size("head")
    group_idx = lax.axis_index("head")
    cycle_len = lax.axis_size("seq")
    cycle_idx = lax.axis_index("seq")
    per_seq = cycle_len // SEQS
    heads_here = HEADS // groups
    width_here = heads_here * HEAD_DIM
    local_len = tokens * groups
    cycle_place = cycle_idx // SEQS
    seq_id = cycle_idx % SEQS
    seq_onehot = jnp.arange(SEQS) == seq_id
    seq_valid = jnp.sum(jnp.where(seq_onehot, lengths, 0))
    is_start = cycle_place == 0
    is_last = cycle_place == per_seq - 1
    first_slot = cycle_place * local_len
    valid_heads = (first_slot + jnp.arange(local_len) < seq_valid).astype(jnp.float32)
    valid_tokens = (first_slot + group_idx * tokens + jnp.arange(tokens) < seq_valid).astype(
        jnp.float32
    )
    source = block_in.astype(jnp.float32)
    in_scale = inverse_rms(source)
    normed = (source * in_scale * norm_gain).astype(jnp.bfloat16)
    projected = jnp.dot(normed, w_in, preferred_element_type=jnp.float32).astype(jnp.bfloat16)
    gate_in = projected[:, :INNER].astype(jnp.float32)
    x_part = projected[:, INNER : 2 * INNER].reshape(tokens, groups, width_here)
    bc_part = jnp.broadcast_to(
        projected[:, None, 2 * INNER : 2 * INNER + 2 * STATE], (tokens, groups, 2 * STATE)
    )
    dt_part = projected[:, 2 * INNER + 2 * STATE :].reshape(tokens, groups, heads_here)
    x_raw, bc_raw, dt_raw = (
        lax.all_to_all(x_part, "head", split_axis=1, concat_axis=0, tiled=True),
        lax.all_to_all(bc_part, "head", split_axis=1, concat_axis=0, tiled=True),
        lax.all_to_all(dt_part, "head", split_axis=1, concat_axis=0, tiled=True),
    )
    x_raw = x_raw.reshape(local_len, width_here)
    bc_raw = bc_raw.reshape(local_len, 2 * STATE)
    dt_raw = dt_raw.reshape(local_len, heads_here).astype(jnp.float32)
    tail = local_len - CONV + 1
    edge_x, edge_bc = passed_along((x_raw[tail:], bc_raw[tail:]), "seq", SEQS)
    edge_keep = jnp.where(is_start, 0.0, 1.0)
    edge_x = edge_x.astype(jnp.float32) * edge_keep
    edge_bc = edge_bc.astype(jnp.float32) * edge_keep
    x_raw = x_raw.astype(jnp.float32)
    bc_raw = bc_raw.astype(jnp.float32)
    conv_x = lax.dynamic_slice_in_dim(conv_w, group_idx * width_here, width_here, 1)
    conv_bc = conv_w[:, INNER:]
    bias_x = lax.dynamic_slice_in_dim(conv_b, group_idx * width_here, width_here, 0)
    bias_bc = conv_b[INNER:]
    dt_shift = lax.dynamic_slice_in_dim(dt_bias, group_idx * heads_here, heads_here, 0)
    a_log_part = lax.dynamic_slice_in_dim(a_log, group_idx * heads_here, heads_here, 0)
    skip_part = lax.dynamic_slice_in_dim(d_skip, group_idx * heads_here, heads_here, 0)
    x_heads, b_rows, c_rows, dt_rows, rates = prepare(
        x_raw,
        bc_raw,
        dt_raw,
        edge_x,
        edge_bc,
        conv_x,
        conv_bc,
        bias_x,
        bias_bc,
        dt_shift,
        a_log_part,
        valid_heads,
    )
    cumulative = jnp.cumsum(dt_rows, axis=0) * rates
    decay_all = jnp.exp(cumulative[-1])
    to_end = jnp.exp(cumulative[-1:] - cumulative) * dt_rows
    own_state = jnp.einsum("uh,uhp,un->hpn", to_end, x_heads, b_rows, precision=best)
    slot_mask = seq_onehot.astype(jnp.float32)
    identity = (
        jnp.ones((SEQS, heads_here), jnp.float32),
        jnp.zeros((SEQS, heads_here, HEAD_DIM, STATE), jnp.float32),
    )

    def slotted(decay_vec, piece_state):
        decay_slots = jnp.where(seq_onehot[:, None], decay_vec[None, :], 1.0)
        state_slots = slot_mask[:, None, None, None] * piece_state[None]
        return (decay_slots, state_slots)

    arrived_all = entering(
        slotted(jnp.where(is_start, 0.0, decay_all), own_state), "seq", chain, identity, False
    )[1]
    arrived = lax.dynamic_index_in_dim(arrived_all, seq_id, 0, keepdims=False)
    incoming = jnp.where(is_start, 0.0, arrived)
    (mixed_heads, final_state), pull_back = jax.vjp(
        partial(mixer, valid_heads),
        x_raw,
        bc_raw,
        dt_raw,
        edge_x,
        edge_bc,
        conv_x,
        conv_bc,
        bias_x,
        bias_bc,
        dt_shift,
        a_log_part,
        skip_part,
        incoming,
    )
    mixed_send = mixed_heads.astype(jnp.bfloat16).reshape(local_len, 1, width_here)
    mixed_tok = (
        lax.all_to_all(mixed_send, "head", split_axis=0, concat_axis=1, tiled=True)
        .reshape(tokens, INNER)
        .astype(jnp.float32)
    )
    gate_sigmoid = jax.nn.sigmoid(gate_in)
    gate_act = gate_in * gate_sigmoid
    gated = mixed_tok * gate_act
    gate_scale = inverse_rms(gated)
    gnormed = (gated * gate_scale * gate_gain).astype(jnp.bfloat16)
    branch = jnp.dot(gnormed, w_out, preferred_element_type=jnp.float32)
    valid_col = valid_tokens[:, None]
    block_out = (source + valid_col * branch).astype(jnp.bfloat16)
    grad_rows = grad_out.astype(jnp.float32)
    d_branch = (grad_rows * valid_col).astype(jnp.bfloat16)
    grad_w_out = jnp.einsum("ti,td->id", gnormed, d_branch, preferred_element_type=jnp.float32)
    d_gnormed = jnp.einsum("td,id->ti", d_branch, w_out, preferred_element_type=jnp.float32)
    d_gated, grad_gate = norm_backward(gated, gate_scale, gate_gain, d_gnormed)
    d_mixed = (d_gated * gate_act).astype(jnp.bfloat16)
    d_gate_in = d_gated * mixed_tok * gate_sigmoid * (1.0 + gate_in * (1.0 - gate_sigmoid))
    d_heads = lax.all_to_all(
        d_mixed.reshape(tokens, groups, width_here), "head", split_axis=1, concat_axis=0, tiled=True
    )
    d_heads = d_heads.reshape(local_len, width_here).astype(jnp.float32)
    weighted = d_heads.reshape(local_len, heads_here, HEAD_DIM) * jnp.exp(cumulative)[:, :, None]
    own_grad = jnp.einsum("thp,tn->hpn", weighted, c_rows, precision=best)
    behind_all = entering(
        slotted(jnp.where(is_last, 0.0, decay_all), own_grad), "seq", chain, identity, True
    )[1]
    behind = lax.dynamic_index_in_dim(behind_all, seq_id, 0, keepdims=False)
    from_right = jnp.where(is_last, 0.0, behind)
    grads = pull_back((d_heads, from_right))
    back_x, back_bc = passed_along((grads[3] * edge_keep, grads[4] * edge_keep), "seq", -SEQS)
    dx_heads = jnp.concatenate([grads[0][:tail], grads[0][tail:] + back_x], axis=0)
    dbc_heads = jnp.concatenate([grads[1][:tail], grads[1][tail:] + back_bc], axis=0)
    rec_x, rec_bc, rec_dt = (
        lax.all_to_all(
            dx_heads.reshape(local_len, 1, width_here),
            "head",
            split_axis=0,
            concat_axis=1,
            tiled=True,
        ),
        lax.all_to_all(
            dbc_heads.reshape(local_len, 1, 2 * STATE),
            "head",
            split_axis=0,
            concat_axis=1,
            tiled=True,
        ),
        lax.all_to_all(
            grads[2].reshape(local_len, 1, heads_here),
            "head",
            split_axis=0,
            concat_axis=1,
            tiled=True,
        ),
    )
    d_projected = jnp.concatenate(
        [
            d_gate_in,
            rec_x.reshape(tokens, INNER),
            jnp.sum(rec_bc, axis=1),
            rec_dt.reshape(tokens, HEADS),
        ],
        axis=1,
    ).astype(jnp.bfloat16)
    grad_w_in = jnp.einsum("td,tp->dp", normed, d_projected, preferred_element_type=jnp.float32)
    d_normed = jnp.einsum("tp,dp->td", d_projected, w_in, preferred_element_type=jnp.float32)
    d_source, grad_norm = norm_backward(source, in_scale, norm_gain, d_normed)
    grad_in = grad_rows + d_source
    grad_conv = jnp.concatenate(
        [place_into(grads[5], INNER, group_idx * width_here), grads[6]], axis=1
    )
    grad_bias = jnp.concatenate(
        [place_into(grads[7], INNER, group_idx * width_here), grads[8]], axis=0
    )
    grad_dt = place_into(grads[9], HEADS, group_idx * heads_here)
    grad_alog = place_into(grads[10], HEADS, group_idx * heads_here)
    grad_skip = place_into(grads[11], HEADS, group_idx * heads_here)
    (
        grad_norm,
        grad_w_in,
        grad_conv,
        grad_bias,
        grad_dt,
        grad_alog,
        grad_skip,
        grad_gate,
        grad_w_out,
    ) = lax.psum(
        (
            grad_norm,
            grad_w_in,
            grad_conv,
            grad_bias,
            grad_dt,
            grad_alog,
            grad_skip,
            grad_gate,
            grad_w_out,
        ),
        ("seq", "head"),
    )
    return (
        block_out,
        grad_in,
        grad_norm,
        grad_w_in,
        grad_conv,
        grad_bias,
        grad_dt,
        grad_alog,
        grad_skip,
        grad_gate,
        grad_w_out,
    )


def solution(mesh):
    placed = (
        P(("seq", "head"), None),
        P(("seq", "head"), None),
        P(),
        P(),
        P(),
        P(),
        P(),
        P(),
        P(),
        P(),
        P(),
        P(),
    )
    return jax.shard_map(
        local,
        mesh=mesh,
        in_specs=placed,
        out_specs=(
            P(("seq", "head"), None),
            P(("seq", "head"), None),
            P(),
            P(),
            P(),
            P(),
            P(),
            P(),
            P(),
            P(),
            P(),
        ),
        check_vma=False,
    )
```

profile of v0, /device:TPU:0, one launch (start us, length us, event | category | flops | bytes accessed | tf_op | source)
XLA Modules:
  0.0 1019.1 jit_solution(1937852641391881275)
XLA Ops:
  9.1 4.2 convolution_convert_fusion
  15.8 5.6 all_to_all.103
  22.0 5.5 collective-permute-start
  70.4 37.2 %all_gather.16 = f32[16,2,12]{2,1,0:T(2,128)S(1)} all-gather(f32[1,2,12]{2,1,0:T(2,128)S(1)} %get-tuple-element.2016), channel_id=1, replica_groups=mesh['seq'=16,'head'=2] {'seq'}, dimensions={0}, use_global_device_ids=true | all-gather | bytes 1632 | tf_op jit(solution)/shard_map/all_gather | solution.py:28
  118.3 102.5 %all-gather.3.cloned.1.call-done = f32[16,2,12,64,128]{4,3,2,1,0:T(8,128)} async-done(((f32[1,2,12,64,128]{4,3,2,1,0:T(8,128)}), f32[16,2,12,64,128]{4,3,2,1,0:T(8,128)}) %all-gather.3.cloned.1.call-update) | async-done | bytes 12582928 | tf_op jit(solution)/shard_map/all_gather | solution.py:28
  224.6 80.5 %while.105 = (s32[]{:T(128)}, f32[12,64,128]{2,1,0:T(8,128)S(1)}, f32[2,256,12,64]{1,0,3,2:T(2,128)}, f32[2,256,12]{1,2,0:T(8,128)S(1)}, f32[2,256,256,12]{2,1,3...) while((s32[]{:T(128)}, f32[12,64,128]{2,1,0:T(8,128)S(1)}, ...), condition=%wide.region_9.10_spmd.clone.clone, body=%wide.region_6.9_spmd.clone.clone.sunk | while | flops 1317872640 | bytes 61413468 | solution.py:139
  235.0 3.8 fusion.240
  239.6 16.7 %dynamic_update_slice.270 = f32[2,256,12,64]{1,0,3,2:T(2,128)} dynamic-update-slice(f32[2,256,12,64]{1,0,3,2:T(2,128)} %get-tuple-element.2536, f32[1,256,12,64]{1,0,3,2:T(1,128)S(1)} %copy.345, s32[]{:T(128)S(6)} %copy.400, s32[]{:T(128)} %constant.277.clone.1..sunk.2, s32[]{:T(128)} %constant.277.clone.1..sunk.2, s32[]{:T(128)} %constant.277.clone.1..sunk.2) | dynamic-update-slice | bytes 1572868 | tf_op jit(solution)/shard_map/jvp()/while/body/jit(dynamic_update_index_in_dim)/dynamic_update_slice | solution.py:139
  256.3 6.3 multiply_dynamic-update-slice_fusion.3
  279.8 16.7 %dynamic_update_slice.270 = f32[2,256,12,64]{1,0,3,2:T(2,128)} dynamic-update-slice(f32[2,256,12,64]{1,0,3,2:T(2,128)} %get-tuple-element.2536, f32[1,256,12,64]{1,0,3,2:T(1,128)S(1)} %copy.345, s32[]{:T(128)S(6)} %copy.400, s32[]{:T(128)} %constant.277.clone.1..sunk.2, s32[]{:T(128)} %constant.277.clone.1..sunk.2, s32[]{:T(128)} %constant.277.clone.1..sunk.2) | dynamic-update-slice | bytes 1572868 | tf_op jit(solution)/shard_map/jvp()/while/body/jit(dynamic_update_index_in_dim)/dynamic_update_slice | solution.py:139
  296.6 6.3 multiply_dynamic-update-slice_fusion.3
  317.8 5.8 all_to_all.104
  340.3 5.4 all_to_all.105
  359.6 58.6 %all_gather.18 = f32[16,2,12]{2,1,0:T(2,128)S(1)} all-gather(f32[1,2,12]{2,1,0:T(2,128)S(1)} %copy-done.141), channel_id=1, replica_groups=mesh['seq'=16,'head'=2] {'seq'}, dimensions={0}, use_global_device_ids=true | all-gather | bytes 1632 | tf_op jit(solution)/shard_map/all_gather | solution.py:28
  421.2 4.5 fusion.160
  425.7 103.9 %all-gather.5.cloned.1.call-done = f32[16,2,12,64,128]{4,3,2,1,0:T(8,128)} async-done(((f32[1,2,12,64,128]{4,3,2,1,0:T(8,128)}), f32[16,2,12,64,128]{4,3,2,1,0:T(8,128)}) %all-gather.5.cloned.1.call-update) | async-done | bytes 12582928 | tf_op jit(solution)/shard_map/all_gather | solution.py:28
  529.6 20.4 %while.104 = (s32[]{:T(128)}, f32[2,12,64,128]{3,2,1,0:T(8,128)S(1)}, s32[]{:T(128)}, f32[16,2,12]{2,1,0:T(2,128)S(1)}, f32[16,2,12,64,128]{4,3,2,1,0:T(8,128)},...) while((s32[]{:T(128)}, f32[2,12,64,128]{3,2,1,0:T(8,128)S(1)}, s32[]{:T(128)}, ...), condition=%wide.region_13.14_spmd, body=%wide.region_12.13_spmd.sunk | while | flops 393222 | bytes 2359739 | solution.py:37
  554.0 121.2 %while.106 = (s32[]{:T(128)}, f32[12]{0:T(128)}, f32[12,64,128]{2,1,0:T(8,128)S(1)}, f32[2,256,12,64]{1,0,3,2:T(2,128)}, f32[2,256,128]{2,1,0:T(8,128)}, /*index...) while((s32[]{:T(128)}, f32[12]{0:T(128)}, ...), condition=%wide.region_25.26_spmd.clone.clone, body=%wide.region_14.25_spmd.clone.clone.sunk | while | flops 2628298752 | bytes 62654428 | solution.py:139
  555.8 9.5 fusion.254
  584.2 4.0 fusion.262
  589.0 16.7 %dynamic_update_slice.275 = f32[2,256,12,64]{1,0,3,2:T(2,128)} dynamic-update-slice(f32[2,256,12,64]{1,0,3,2:T(2,128)} %get-tuple-element.2656, f32[1,256,12,64]{1,0,3,2:T(1,128)S(1)} %copy.348, s32[]{:T(128)S(6)} %sub.279, s32[]{:T(128)} %constant.277.clone.1..sunk.3, s32[]{:T(128)} %constant.277.clone.1..sunk.3, s32[]{:T(128)} %constant.277.clone.1..sunk.3) | dynamic-update-slice | bytes 1572868 | tf_op jit(solution)/shard_map/transpose(jvp())/while/body/jit(dynamic_update_index_in_dim)/dynamic_update_slice | solution.py:139
  616.3 9.5 fusion.254
  644.5 4.0 fusion.262
  649.3 16.7 %dynamic_update_slice.275 = f32[2,256,12,64]{1,0,3,2:T(2,128)} dynamic-update-slice(f32[2,256,12,64]{1,0,3,2:T(2,128)} %get-tuple-element.2656, f32[1,256,12,64]{1,0,3,2:T(1,128)S(1)} %copy.348, s32[]{:T(128)S(6)} %sub.279, s32[]{:T(128)} %constant.277.clone.1..sunk.3, s32[]{:T(128)} %constant.277.clone.1..sunk.3, s32[]{:T(128)} %constant.277.clone.1..sunk.3) | dynamic-update-slice | bytes 1572868 | tf_op jit(solution)/shard_map/transpose(jvp())/while/body/jit(dynamic_update_index_in_dim)/dynamic_update_slice | solution.py:139
  687.1 6.1 multiply_reduce_fusion.3
  711.1 4.2 all_to_all.107
  720.4 5.2 all_to_all.108
  733.0 6.8 fusion.156
  745.8 5.9 fusion.148
  751.7 45.2 %all-reduce.20 = (f32[768]{0:T(1024)}, f32[4,1792]{1,0:T(4,128)}, f32[1792]{0:T(1024)}, f32[24]{0:T(128)}, f32[24]{0:T(128)}, /*index=5*/f32[24]{0:T(128)}, f32[1536]{0:T(1024)}) all-reduce(f32[768]{0:T(1024)S(1)} %get-tuple-element.1806, f32[4,1792]{1,0:T(4,128)S(1)} %pad_maximum_fusion.5, ...), channel_id=1, replica_groups=mesh['seq'=16,'head'=2] {'seq','head'}, use_global_device_ids=true, to_apply=%region_29.30 | all-reduce | flops 11336 | bytes 90688 | tf_op jit(solution)/shard_map/psum | solution.py:366
  799.2 201.9 %all-reduce.24.cloned.1.call-done = (f32[768,3352]{0,1:T(8,128)}, f32[1536,768]{1,0:T(8,128)}) async-done(((f32[768,3352]{0,1:T(8,128)}, f32[1536,768]{1,0:T(8,128)}), (f32[768,3352]{0,1:T(8,128)}, f32[1536,768]{1,0:T(8,128)})) %all-reduce.24.cloned.1.call-update) | async-done | bytes 15015952 | tf_op jit(solution)/shard_map/psum | solution.py:366
  1001.1 8.8 copy.483
  (738 shorter events, 273.9 us)
Async XLA Ops:
  7.2 326.1 %copy-start = (bf16[1536,768]{1,0:T(8,128)(2,1)S(1)}, bf16[1536,768]{1,0:T(8,128)(2,1)}, u32[]{:S(2)}) copy-start(bf16[1536,768]{1,0:T(8,128)(2,1)} %param.31) | copy-start | bytes 7077892
  14.6 12.8 %slice-start = ((bf16[256,3352]{0,1:T(8,128)(2,1)}), bf16[256,256]{0,1:T(8,128)(2,1)S(1)}, s32[]{:S(2)}) async-start(bf16[256,3352]{0,1:T(8,128)(2,1)} %copy-done.40), calls=%async_computation.11 | async-start | bytes 262144 | tf_op jit(solution)/shard_map/slice | solution.py:200
  15.8 16.0 %slice-start.1 = ((bf16[256,3352]{0,1:T(8,128)(2,1)}), bf16[256,24]{0,1:T(8,128)(2,1)S(1)}, s32[]{:S(2)}) async-start(bf16[256,3352]{0,1:T(8,128)(2,1)} %copy-done.40), calls=%async_computation.12 | async-start | bytes 24576 | tf_op jit(solution)/shard_map/slice | solution.py:202
  15.8 25.3 %copy-start.149 = (s32[2]{0:T(128)S(1)}, s32[2]{0:T(128)}, u32[]{:S(2)}) copy-start(s32[2]{0:T(128)} %param.22) | copy-start | bytes 28
  21.4 31.6 %copy-start.28 = (bf16[256,2,768]{2,0,1:T(8,128)(2,1)}, bf16[256,2,768]{2,0,1:T(8,128)(2,1)S(1)}, u32[]{:S(2)}) copy-start(bf16[256,2,768]{2,0,1:T(8,128)(2,1)S(1)} %all_to_all.103) | copy-start | bytes 2359300
  22.0 36.4 %collective-permute-start = (bf16[3,768]{1,0:T(4,128)(2,1)}, bf16[3,768]{1,0:T(4,128)(2,1)}, u32[]{:S(2)}, u32[]{:S(2)}) collective-permute-start(bf16[3,768]{1,0:T(4,128)(2,1)} %slice.198), channel_id=1, source_target_pairs={{0,4},{2,6},{4,8},{6,10},{8,12},{10,14},{12,16},{14,18},{16,20},{1... | collective-permute-start | bytes 13832 | tf_op jit(solution)/shard_map/ppermute | solution.py:21
  28.3 5.0 all-to-all-start.2
  33.3 19.7 %copy-start.46 = (bf16[256,2,256]{2,0,1:T(8,128)(2,1)}, bf16[256,2,256]{2,0,1:T(8,128)(2,1)S(1)}, u32[]{:S(2)}) copy-start(bf16[256,2,256]{2,0,1:T(8,128)(2,1)S(1)} %all-to-all-done.2) | copy-start | bytes 786436
  33.3 8.5 all-to-all-start
  36.5 184.3 %all-gather.3.cloned.1.call-start = ((), (), s32[]{:S(2)}) async-start(), calls=%async_computation.8 | async-start | bytes 13369344 | tf_op jit(solution)/shard_map/all_gather | solution.py:28
  37.2 17.7 %collective-permute-start.1 = (bf16[3,256]{1,0:T(4,128)(2,1)}, bf16[3,256]{1,0:T(4,128)(2,1)}, u32[]{:S(2)}, u32[]{:S(2)}) collective-permute-start(bf16[3,256]{1,0:T(4,128)(2,1)} %slice.204), channel_id=1, source_target_pairs={{0,4},{2,6},{4,8},{6,10},{8,12},{10,14},{12,16},{14,18},{16,20},{1... | collective-permute-start | bytes 4616 | tf_op jit(solution)/shard_map/ppermute | solution.py:21
  41.7 69.1 %copy-start.77 = (bf16[256,2,12]{0,2,1:T(8,128)(2,1)}, bf16[256,2,12]{0,2,1:T(8,128)(2,1)S(1)}, u32[]{:S(2)}) copy-start(bf16[256,2,12]{0,2,1:T(8,128)(2,1)S(1)} %all-to-all-done) | copy-start | bytes 36868
  41.7 11.2 %copy-start.71 = (f32[2,256,1,12]{1,3,0,2:T(8,128)}, f32[2,256,1,12]{1,3,0,2:T(8,128)S(1)}, u32[]{:S(2)}) copy-start(f32[2,256,1,12]{1,3,0,2:T(8,128)S(1)} %convert_bitcast_fusion.3) | copy-start | bytes 73732
  42.5 16.7 %copy-start.91 = (f32[512]{0:T(512)}, f32[512]{0:T(512)S(1)}, u32[]{:S(2)}) copy-start(f32[512]{0:T(512)S(1)} %fusion.181) | copy-start | bytes 6148
  43.2 9.7 copy-start.121
  58.4 53.2 %copy-start.35 = (f32[512,256]{1,0:T(8,128)}, f32[512,256]{1,0:T(8,128)S(1)}, u32[]{:S(2)}) copy-start(f32[512,256]{1,0:T(8,128)S(1)} %get-tuple-element.1976) | copy-start | bytes 1572868
  67.8 39.9 %copy-start.147 = (f32[24]{0:T(128)S(1)}, f32[24]{0:T(128)}, u32[]{:S(2)}) copy-start(f32[24]{0:T(128)} %param.28) | copy-start | bytes 292
  67.8 43.1 %copy-start.122 = (f32[12]{0:T(128)S(1)}, f32[12]{0:T(128)}, u32[]{:S(2)}) copy-start(f32[12]{0:T(128)} %copy-done.121) | copy-start | bytes 148
  68.9 460.7 %all-gather.5.cloned.1.call-start = ((), (), s32[]{:S(2)}) async-start(), calls=%async_computation.9 | async-start | bytes 13369344 | tf_op jit(solution)/shard_map/all_gather | solution.py:28
  333.3 87.9 %copy-start.98 = (f32[256]{0:T(256)}, f32[256]{0:T(256)S(1)}, u32[]{:S(2)}) copy-start(f32[256]{0:T(256)S(1)} %get-tuple-element.2014) | copy-start | bytes 3076
  358.9 642.3 %all-reduce.24.cloned.1.call-start = ((), (), s32[]{:S(2)}) async-start(), calls=%async_computation.10 | async-start | bytes 30031872 | tf_op jit(solution)/shard_map/psum | solution.py:366
  555.8 9.5 copy-start.1
  555.8 9.5 copy-start.21
  555.8 10.2 %copy-start.11 = (f32[2,256,128]{2,1,0:T(8,128)S(1)}, f32[2,256,128]{2,1,0:T(8,128)}, u32[]{:S(2)}) copy-start(f32[2,256,128]{2,1,0:T(8,128)} %get-tuple-element.2697) | copy-start | bytes 786436 | tf_op jit(solution)/shard_map/transpose(jvp())/while
  616.3 9.5 copy-start.1
  616.3 9.5 copy-start.21
  616.3 10.2 %copy-start.11 = (f32[2,256,128]{2,1,0:T(8,128)S(1)}, f32[2,256,128]{2,1,0:T(8,128)}, u32[]{:S(2)}) copy-start(f32[2,256,128]{2,1,0:T(8,128)} %get-tuple-element.2697) | copy-start | bytes 786436 | tf_op jit(solution)/shard_map/transpose(jvp())/while
  680.0 29.8 %collective-permute-start.3 = (f32[3,256]{1,0:T(4,128)}, f32[3,256]{1,0:T(4,128)}, u32[]{:S(2)}, u32[]{:S(2)}) collective-permute-start(f32[3,256]{1,0:T(4,128)} %add_multiply_fusion.1), channel_id=1, source_target_pairs={{4,0},{6,2},{8,4},{10,6},{12,8},{14,10},{16,12},{18,14},{20,16},{2... | collective-permute-start | bytes 9224 | tf_op jit(solution)/shard_map/ppermute | solution.py:21
  706.3 9.8 collective-permute-start.2
  745.8 51.1 %copy-start.43 = (bf16[256,768]{1,0:T(8,128)(2,1)S(1)}, bf16[256,768]{1,0:T(8,128)(2,1)}, u32[]{:S(2)}) copy-start(bf16[256,768]{1,0:T(8,128)(2,1)} %param.21) | copy-start | bytes 1179652
  745.8 51.1 %copy-start.135 = (f32[256]{0:T(256)S(1)}, f32[256]{0:T(256)}, u32[]{:S(2)}) copy-start(f32[256]{0:T(256)} %get-tuple-element.2011) | copy-start | bytes 3076
  1001.1 8.8 copy-start.34
  (179 other events, 671.6 us)
Sparse Core Ops, SparseCore 0:
  69.0 151.7 all-gather.2
  359.0 170.5 all-gather.4
  740.0 261.1 all-reduce.23
where the time goes:
time: 1030 us; the launch traced here: 1020 us
  waiting for transfers between devices  409 us (40%)
  local copies, waits for them, and re-layouts  185 us (18%)
  blocking collectives  171 us (17%)
  other arithmetic  118 us (11%)
  matrix products  99.5 us (10%)
  starting transfers between devices  18.3 us (2%)
  between operations  15.6 us (2%)
    all_gather x2, waiting for transfers between devices, entering(): gathered = jax.tree.map(lambda a: lax.all_gather(a, axis), part)  206 us
    psum x1, waiting for transfers between devices, local(): lax.psum((grad_norm, grad_w_in, grad_conv, grad_bias, grad_dt, grad_alog,...  202 us
    all_gather x2, blocking collectives, entering(): gathered = jax.tree.map(lambda a: lax.all_gather(a, axis), part)  95.8 us
    dynamic_update_slice x18, local copies, waits for them, and re-layouts, mixer(): lax.scan(partial(block_step, rates), incoming, (blocks(x_heads), blocks(b...  71.9 us
    psum x1, blocking collectives, local(): lax.psum((grad_norm, grad_w_in, grad_conv, grad_bias, grad_dt, grad_alog,...  45.2 us
    dot_general x6, matrix products, block_step(): inner_part = jnp.einsum('tuh,uhp->thp', weight, x_heads, precision=best)  34.4 us
    unnamed x229, local copies, waits for them, and re-layouts  32.9 us
  transfers between devices with their start and end apart: 9, of which 4 were waited for; matrix products, arithmetic and copies ran while one was open for 8% of the time, Pallas kernels for 0%

commit v1 on v0

--- a/solution.py
+++ b/solution.py
@@ -13,6 +13,11 @@
 SEQS = 2
 eps_norm = 1e-05
 best = lax.Precision.HIGHEST
+
+
+def one_after_other(x, one_2, other):
+    inner = lax.psum(x, one_2)
+    return lax.psum(inner, other)
 
 
 def passed_along(value, axis, steps):
@@ -363,7 +368,7 @@
         grad_skip,
         grad_gate,
         grad_w_out,
-    ) = lax.psum(
+    ) = one_after_other(
         (
             grad_norm,
             grad_w_in,
@@ -375,7 +380,8 @@
             grad_gate,
             grad_w_out,
         ),
-        ("seq", "head"),
+        "head",
+        "seq",
     )
     return (
         block_out,

time: 1030 us -> 1250 us (1.21)
  waiting for transfers between devices: 409 us -> 588 us
  blocking collectives: 171 us -> 212 us
    psum x1 -> x2, waiting for transfers between devices: 202 us -> 381 us  [the longest x1 326 us: one_after_other(): return lax.psum(inner, other)]
    psum x1 -> x2, blocking collectives: 45.2 us -> 86.2 us  [the longest x1 82.6 us: one_after_other(): return lax.psum(inner, other)]
  transfers between devices with their start and end apart: 9 -> 10, of which waited for: 4 -> 5; matrix products, arithmetic and copies ran while one was open for 8% -> 6% of each run, Pallas kernels for 0% -> 0%
where the time goes in v1:
time: 1250 us; the launch traced here: 1240 us
  waiting for transfers between devices  588 us (47%)
  blocking collectives  212 us (17%)
  local copies, waits for them, and re-layouts  185 us (15%)
  other arithmetic  118 us (9%)
  matrix products  99.2 us (8%)
  starting transfers between devices  18.3 us (1%)
  between operations  15.6 us (1%)
    psum x1, waiting for transfers between devices, one_after_other(): return lax.psum(inner, other)  326 us
    all_gather x2, waiting for transfers between devices, entering(): gathered = jax.tree.map(lambda a: lax.all_gather(a, axis), part)  206 us
    all_gather x2, blocking collectives, entering(): gathered = jax.tree.map(lambda a: lax.all_gather(a, axis), part)  95.8 us
    psum x1, blocking collectives, one_after_other(): return lax.psum(inner, other)  82.6 us
    dynamic_update_slice x18, local copies, waits for them, and re-layouts, mixer(): lax.scan(partial(block_step, rates), incoming, (blocks(x_heads), blocks(b...  71.9 us
    psum x1, waiting for transfers between devices, one_after_other(): inner = lax.psum(x, one_2)  54.5 us
    dot_general x6, matrix products, block_step(): inner_part = jnp.einsum('tuh,uhp->thp', weight, x_heads, precision=best)  34.4 us
    unnamed x229, local copies, waits for them, and re-layouts  32.9 us
  transfers between devices with their start and end apart: 10, of which 5 were waited for; matrix products, arithmetic and copies ran while one was open for 6% of the time, Pallas kernels for 0%

profile of v1, /device:TPU:0, one launch (start us, length us, event | category | flops | bytes accessed | tf_op | source)
XLA Modules:
  0.0 1238.9 jit_solution(9972777307855817055)
XLA Ops:
  9.1 4.2 convolution_convert_fusion
  15.8 5.6 all_to_all.103
  22.0 5.5 collective-permute-start
  70.4 37.2 %all_gather.16 = f32[16,2,12]{2,1,0:T(2,128)S(1)} all-gather(f32[1,2,12]{2,1,0:T(2,128)S(1)} %get-tuple-element.2025), channel_id=1, replica_groups=mesh['seq'=16,'head'=2] {'seq'}, dimensions={0}, use_global_device_ids=true | all-gather | bytes 1632 | tf_op jit(solution)/shard_map/all_gather | solution.py:33
  118.3 102.5 %all-gather.3.cloned.1.call-done = f32[16,2,12,64,128]{4,3,2,1,0:T(8,128)} async-done(((f32[1,2,12,64,128]{4,3,2,1,0:T(8,128)}), f32[16,2,12,64,128]{4,3,2,1,0:T(8,128)}) %all-gather.3.cloned.1.call-update) | async-done | bytes 12582928 | tf_op jit(solution)/shard_map/all_gather | solution.py:33
  224.6 80.5 %while.105 = (s32[]{:T(128)}, f32[12,64,128]{2,1,0:T(8,128)S(1)}, f32[2,256,12,64]{1,0,3,2:T(2,128)}, f32[2,256,12]{1,2,0:T(8,128)S(1)}, f32[2,256,256,12]{2,1,3...) while((s32[]{:T(128)}, f32[12,64,128]{2,1,0:T(8,128)S(1)}, ...), condition=%wide.region_9.10_spmd.clone.clone, body=%wide.region_6.9_spmd.clone.clone.sunk | while | flops 1317872640 | bytes 61413468 | solution.py:144
  239.6 16.7 %dynamic_update_slice.270 = f32[2,256,12,64]{1,0,3,2:T(2,128)} dynamic-update-slice(f32[2,256,12,64]{1,0,3,2:T(2,128)} %get-tuple-element.2545, f32[1,256,12,64]{1,0,3,2:T(1,128)S(1)} %copy.345, s32[]{:T(128)S(6)} %copy.400, s32[]{:T(128)} %constant.277.clone.1..sunk.2, s32[]{:T(128)} %constant.277.clone.1..sunk.2, s32[]{:T(128)} %constant.277.clone.1..sunk.2) | dynamic-update-slice | bytes 1572868 | tf_op jit(solution)/shard_map/jvp()/while/body/jit(dynamic_update_index_in_dim)/dynamic_update_slice | solution.py:144
  256.3 6.3 multiply_dynamic-update-slice_fusion.3
  279.8 16.7 %dynamic_update_slice.270 = f32[2,256,12,64]{1,0,3,2:T(2,128)} dynamic-update-slice(f32[2,256,12,64]{1,0,3,2:T(2,128)} %get-tuple-element.2545, f32[1,256,12,64]{1,0,3,2:T(1,128)S(1)} %copy.345, s32[]{:T(128)S(6)} %copy.400, s32[]{:T(128)} %constant.277.clone.1..sunk.2, s32[]{:T(128)} %constant.277.clone.1..sunk.2, s32[]{:T(128)} %constant.277.clone.1..sunk.2) | dynamic-update-slice | bytes 1572868 | tf_op jit(solution)/shard_map/jvp()/while/body/jit(dynamic_update_index_in_dim)/dynamic_update_slice | solution.py:144
  296.6 6.3 multiply_dynamic-update-slice_fusion.3
  317.8 5.8 all_to_all.104
  340.3 5.4 all_to_all.105
  359.6 58.6 %all_gather.18 = f32[16,2,12]{2,1,0:T(2,128)S(1)} all-gather(f32[1,2,12]{2,1,0:T(2,128)S(1)} %copy-done.141), channel_id=1, replica_groups=mesh['seq'=16,'head'=2] {'seq'}, dimensions={0}, use_global_device_ids=true | all-gather | bytes 1632 | tf_op jit(solution)/shard_map/all_gather | solution.py:33
  421.2 4.5 fusion.160
  425.7 103.9 %all-gather.5.cloned.1.call-done = f32[16,2,12,64,128]{4,3,2,1,0:T(8,128)} async-done(((f32[1,2,12,64,128]{4,3,2,1,0:T(8,128)}), f32[16,2,12,64,128]{4,3,2,1,0:T(8,128)}) %all-gather.5.cloned.1.call-update) | async-done | bytes 12582928 | tf_op jit(solution)/shard_map/all_gather | solution.py:33
  529.6 20.4 %while.104 = (s32[]{:T(128)}, f32[2,12,64,128]{3,2,1,0:T(8,128)S(1)}, s32[]{:T(128)}, f32[16,2,12]{2,1,0:T(2,128)S(1)}, f32[16,2,12,64,128]{4,3,2,1,0:T(8,128)},...) while((s32[]{:T(128)}, f32[2,12,64,128]{3,2,1,0:T(8,128)S(1)}, s32[]{:T(128)}, ...), condition=%wide.region_13.14_spmd, body=%wide.region_12.13_spmd.sunk | while | flops 393222 | bytes 2359739 | solution.py:42
  554.0 121.2 %while.106 = (s32[]{:T(128)}, f32[12]{0:T(128)}, f32[12,64,128]{2,1,0:T(8,128)S(1)}, f32[2,256,12,64]{1,0,3,2:T(2,128)}, f32[2,256,128]{2,1,0:T(8,128)}, /*index...) while((s32[]{:T(128)}, f32[12]{0:T(128)}, ...), condition=%wide.region_25.26_spmd.clone.clone, body=%wide.region_14.25_spmd.clone.clone.sunk | while | flops 2628298752 | bytes 62654428 | solution.py:144
  555.8 9.5 fusion.254
  584.2 4.0 fusion.262
  589.0 16.7 %dynamic_update_slice.275 = f32[2,256,12,64]{1,0,3,2:T(2,128)} dynamic-update-slice(f32[2,256,12,64]{1,0,3,2:T(2,128)} %get-tuple-element.2665, f32[1,256,12,64]{1,0,3,2:T(1,128)S(1)} %copy.348, s32[]{:T(128)S(6)} %sub.279, s32[]{:T(128)} %constant.277.clone.1..sunk.3, s32[]{:T(128)} %constant.277.clone.1..sunk.3, s32[]{:T(128)} %constant.277.clone.1..sunk.3) | dynamic-update-slice | bytes 1572868 | tf_op jit(solution)/shard_map/transpose(jvp())/while/body/jit(dynamic_update_index_in_dim)/dynamic_update_slice | solution.py:144
  616.3 9.5 fusion.254
  644.5 4.0 fusion.262
  649.3 16.7 %dynamic_update_slice.275 = f32[2,256,12,64]{1,0,3,2:T(2,128)} dynamic-update-slice(f32[2,256,12,64]{1,0,3,2:T(2,128)} %get-tuple-element.2665, f32[1,256,12,64]{1,0,3,2:T(1,128)S(1)} %copy.348, s32[]{:T(128)S(6)} %sub.279, s32[]{:T(128)} %constant.277.clone.1..sunk.3, s32[]{:T(128)} %constant.277.clone.1..sunk.3, s32[]{:T(128)} %constant.277.clone.1..sunk.3) | dynamic-update-slice | bytes 1572868 | tf_op jit(solution)/shard_map/transpose(jvp())/while/body/jit(dynamic_update_index_in_dim)/dynamic_update_slice | solution.py:144
  687.1 6.1 multiply_reduce_fusion.3
  711.1 4.2 all_to_all.107
  720.4 5.2 all_to_all.108
  733.0 6.8 fusion.156
  739.9 54.5 %all-reduce.29.cloned.1.call-done = (f32[768,3352]{0,1:T(8,128)}, f32[1536,768]{1,0:T(8,128)}) async-done(((f32[768,3352]{0,1:T(8,128)}, f32[1536,768]{1,0:T(8,128)}), (f32[768,3352]{0,1:T(8,128)}, f32[1536,768]{1,0:T(8,128)})) %all-reduce.29.cloned.1.call-update) | async-done | bytes 15015952 | tf_op jit(solution)/shard_map/psum | solution.py:19
  800.3 5.6 fusion.148
  809.6 82.6 %all-reduce.20 = (f32[768]{0:T(1024)}, f32[4,1792]{1,0:T(4,128)}, f32[1792]{0:T(1024)}, f32[24]{0:T(128)}, f32[24]{0:T(128)}, /*index=5*/f32[24]{0:T(128)}, f32[1536]{0:T(1024)}) all-reduce(f32[768]{0:T(1024)S(1)} %get-tuple-element.1963, f32[4,1792]{1,0:T(4,128)S(1)} %get-tuple-element.1964, ...), channel_id=1, replica_groups=mesh['seq'=16,'head'=2] {'seq'}, use_global_device_ids=true, to_apply=%region_30.31 | all-reduce | flops 11336 | bytes 90688 | tf_op jit(solution)/shard_map/psum | solution.py:20
  894.5 326.4 %all-reduce.27.cloned.1.call-done = (f32[768,3352]{0,1:T(8,128)}, f32[1536,768]{1,0:T(8,128)}) async-done(((f32[768,3352]{0,1:T(8,128)}, f32[1536,768]{1,0:T(8,128)}), (f32[768,3352]{0,1:T(8,128)}, f32[1536,768]{1,0:T(8,128)})) %all-reduce.27.cloned.1.call-update) | async-done | bytes 15015952 | tf_op jit(solution)/shard_map/psum | solution.py:20
  1220.9 8.8 copy.485
  (742 shorter events, 281.4 us)
Async XLA Ops:
  7.2 326.1 %copy-start = (bf16[1536,768]{1,0:T(8,128)(2,1)S(1)}, bf16[1536,768]{1,0:T(8,128)(2,1)}, u32[]{:S(2)}) copy-start(bf16[1536,768]{1,0:T(8,128)(2,1)} %param.31) | copy-start | bytes 7077892
  14.6 12.8 %slice-start = ((bf16[256,3352]{0,1:T(8,128)(2,1)}), bf16[256,256]{0,1:T(8,128)(2,1)S(1)}, s32[]{:S(2)}) async-start(bf16[256,3352]{0,1:T(8,128)(2,1)} %copy-done.40), calls=%async_computation.12 | async-start | bytes 262144 | tf_op jit(solution)/shard_map/slice | solution.py:205
  15.8 16.0 %slice-start.1 = ((bf16[256,3352]{0,1:T(8,128)(2,1)}), bf16[256,24]{0,1:T(8,128)(2,1)S(1)}, s32[]{:S(2)}) async-start(bf16[256,3352]{0,1:T(8,128)(2,1)} %copy-done.40), calls=%async_computation.13 | async-start | bytes 24576 | tf_op jit(solution)/shard_map/slice | solution.py:207
  15.8 25.3 %copy-start.149 = (s32[2]{0:T(128)S(1)}, s32[2]{0:T(128)}, u32[]{:S(2)}) copy-start(s32[2]{0:T(128)} %param.22) | copy-start | bytes 28
  21.4 31.6 %copy-start.28 = (bf16[256,2,768]{2,0,1:T(8,128)(2,1)}, bf16[256,2,768]{2,0,1:T(8,128)(2,1)S(1)}, u32[]{:S(2)}) copy-start(bf16[256,2,768]{2,0,1:T(8,128)(2,1)S(1)} %all_to_all.103) | copy-start | bytes 2359300
  22.0 36.4 %collective-permute-start = (bf16[3,768]{1,0:T(4,128)(2,1)}, bf16[3,768]{1,0:T(4,128)(2,1)}, u32[]{:S(2)}, u32[]{:S(2)}) collective-permute-start(bf16[3,768]{1,0:T(4,128)(2,1)} %slice.198), channel_id=1, source_target_pairs={{0,4},{2,6},{4,8},{6,10},{8,12},{10,14},{12,16},{14,18},{16,20},{1... | collective-permute-start | bytes 13832 | tf_op jit(solution)/shard_map/ppermute | solution.py:26
  28.3 5.0 all-to-all-start.2
  33.3 19.7 %copy-start.46 = (bf16[256,2,256]{2,0,1:T(8,128)(2,1)}, bf16[256,2,256]{2,0,1:T(8,128)(2,1)S(1)}, u32[]{:S(2)}) copy-start(bf16[256,2,256]{2,0,1:T(8,128)(2,1)S(1)} %all-to-all-done.2) | copy-start | bytes 786436
  33.3 8.5 all-to-all-start
  36.5 184.3 %all-gather.3.cloned.1.call-start = ((), (), s32[]{:S(2)}) async-start(), calls=%async_computation.8 | async-start | bytes 13369344 | tf_op jit(solution)/shard_map/all_gather | solution.py:33
  37.2 17.7 %collective-permute-start.1 = (bf16[3,256]{1,0:T(4,128)(2,1)}, bf16[3,256]{1,0:T(4,128)(2,1)}, u32[]{:S(2)}, u32[]{:S(2)}) collective-permute-start(bf16[3,256]{1,0:T(4,128)(2,1)} %slice.204), channel_id=1, source_target_pairs={{0,4},{2,6},{4,8},{6,10},{8,12},{10,14},{12,16},{14,18},{16,20},{1... | collective-permute-start | bytes 4616 | tf_op jit(solution)/shard_map/ppermute | solution.py:26
  41.7 69.1 %copy-start.77 = (bf16[256,2,12]{0,2,1:T(8,128)(2,1)}, bf16[256,2,12]{0,2,1:T(8,128)(2,1)S(1)}, u32[]{:S(2)}) copy-start(bf16[256,2,12]{0,2,1:T(8,128)(2,1)S(1)} %all-to-all-done) | copy-start | bytes 36868
  41.7 11.2 copy-start.71
  42.5 16.7 %copy-start.91 = (f32[512]{0:T(512)}, f32[512]{0:T(512)S(1)}, u32[]{:S(2)}) copy-start(f32[512]{0:T(512)S(1)} %fusion.181) | copy-start | bytes 6148
  43.2 9.7 copy-start.121
  58.4 53.2 %copy-start.35 = (f32[512,256]{1,0:T(8,128)}, f32[512,256]{1,0:T(8,128)S(1)}, u32[]{:S(2)}) copy-start(f32[512,256]{1,0:T(8,128)S(1)} %get-tuple-element.1985) | copy-start | bytes 1572868
  67.8 39.9 %copy-start.147 = (f32[24]{0:T(128)S(1)}, f32[24]{0:T(128)}, u32[]{:S(2)}) copy-start(f32[24]{0:T(128)} %param.28) | copy-start | bytes 292
  67.8 43.1 %copy-start.122 = (f32[12]{0:T(128)S(1)}, f32[12]{0:T(128)}, u32[]{:S(2)}) copy-start(f32[12]{0:T(128)} %copy-done.121) | copy-start | bytes 148
  68.9 460.7 %all-gather.5.cloned.1.call-start = ((), (), s32[]{:S(2)}) async-start(), calls=%async_computation.9 | async-start | bytes 13369344 | tf_op jit(solution)/shard_map/all_gather | solution.py:33
  333.3 87.9 %copy-start.98 = (f32[256]{0:T(256)}, f32[256]{0:T(256)S(1)}, u32[]{:S(2)}) copy-start(f32[256]{0:T(256)S(1)} %get-tuple-element.2023) | copy-start | bytes 3076
  358.9 435.5 %all-reduce.29.cloned.1.call-start = ((), (), s32[]{:S(2)}) async-start(), calls=%async_computation.11 | async-start | bytes 30031872 | tf_op jit(solution)/shard_map/psum | solution.py:19
  555.8 9.5 copy-start.1
  555.8 9.5 copy-start.21
  555.8 10.2 copy-start.11
  616.3 9.5 copy-start.1
  616.3 9.5 copy-start.21
  616.3 10.2 copy-start.11
  680.0 29.8 %collective-permute-start.3 = (f32[3,256]{1,0:T(4,128)}, f32[3,256]{1,0:T(4,128)}, u32[]{:S(2)}, u32[]{:S(2)}) collective-permute-start(f32[3,256]{1,0:T(4,128)} %add_multiply_fusion.1), channel_id=1, source_target_pairs={{4,0},{6,2},{8,4},{10,6},{12,8},{14,10},{16,12},{18,14},{20,16},{2... | collective-permute-start | bytes 9224 | tf_op jit(solution)/shard_map/ppermute | solution.py:26
  706.3 9.8 collective-permute-start.2
  739.8 481.1 %all-reduce.27.cloned.1.call-start = ((), (), s32[]{:S(2)}) async-start(), calls=%async_computation.10 | async-start | bytes 30031872 | tf_op jit(solution)/shard_map/psum | solution.py:20
  800.3 91.9 %copy-start.43 = (bf16[256,768]{1,0:T(8,128)(2,1)S(1)}, bf16[256,768]{1,0:T(8,128)(2,1)}, u32[]{:S(2)}) copy-start(bf16[256,768]{1,0:T(8,128)(2,1)} %param.21) | copy-start | bytes 1179652
  800.3 91.9 %copy-start.135 = (f32[256]{0:T(256)S(1)}, f32[256]{0:T(256)}, u32[]{:S(2)}) copy-start(f32[256]{0:T(256)} %get-tuple-element.2020) | copy-start | bytes 3076
  (180 other events, 680.1 us)
Sparse Core Ops, SparseCore 0:
  69.0 151.7 all-gather.2
  359.0 170.5 all-gather.4
  740.0 54.3 all-reduce.28
  801.8 419.1 all-reduce.26
